TPU v7x, 128 devices: a whole 4x4x4 slice. The times are simulated.
128 devices in a mesh: gx: 16 (over x_hi, z, core), gy: 8 (over x_lo, y).
Axes of the slice: x: 4 (x_hi: 2, x_lo: 2; x = x_hi * 2 + x_lo), y: 4, z: 4, core: 2. Of those that a mesh axis runs over, the one named last changes fastest.
Arguments:
- populations: float32 [19, 256, 128, 128], P(None, 'gx', 'gy')
- panels: bfloat16 [64, 200, 128], P(None, None, ('gx', 'gy')), may hold values from -0.59765625 to 0.59765625
- modal_vel: bfloat16 [64, 2, 200], replicated, may hold values from -0.4375 to 0.4375
- marker_x: int32 [16, 8, 512], P('gx', 'gy'), may hold values from 0 to 15
- marker_y: int32 [16, 8, 512], P('gx', 'gy'), may hold values from 0 to 15
- marker_z: int32 [16, 8, 512], P('gx', 'gy'), may hold values from 0 to 127
- marker_riser: int32 [16, 8, 512], P('gx', 'gy'), may hold values from 0 to 63
Outputs:
- next_populations: float32 [19, 256, 128, 128], P(None, 'gx', 'gy')
- marker_force: float32 [16, 8, 3, 512], P('gx', 'gy')
- force_field: float32 [3, 256, 128, 128], P(None, 'gx', 'gy')
All inputs are finite; a program needn't handle non-finite values.
Results may differ from a plain program's by a relative error of at most 0.0008.
Values may be sent and summed in bfloat16 or wider, within the bound.
No kernel may reach another device: no remote copies, remote signals or barrier semaphores. Data moves between devices by JAX's collectives and lax.ppermute only.
A program may use at most 128 MiB of HBM per device.

v0:
```python
import jax
import jax.numpy as jnp
from jax import lax
from jax.sharding import PartitionSpec as P

VELOCITY = (
    (0, 0, 0),
    (1, 0, 0),
    (-1, 0, 0),
    (0, 1, 0),
    (0, -1, 0),
    (0, 0, 1),
    (0, 0, -1),
    (1, 1, 0),
    (-1, -1, 0),
    (1, -1, 0),
    (-1, 1, 0),
    (1, 0, 1),
    (-1, 0, -1),
    (1, 0, -1),
    (-1, 0, 1),
    (0, 1, 1),
    (0, -1, -1),
    (0, 1, -1),
    (0, -1, 1),
)
WEIGHT = (1.0 / 3.0,) + (1.0 / 18.0,) * 6 + (1.0 / 36.0,) * 12
KERNEL = (0.25, 0.5, 0.25)
RELAX = 0.8


def extended(shard, sides, width):
    for axis, dim in sides:
        devices, length = (lax.axis_size(axis), shard.shape[dim])
        up = [(i, (i + 1) % devices) for i in range(devices)]
        down = [(j, i) for i, j in up]
        last = lax.slice_in_dim(shard, length - width, length, axis=dim)
        first = lax.slice_in_dim(shard, 0, width, axis=dim)
        before = lax.ppermute(last, axis, up)
        after = lax.ppermute(first, axis, down)
        shard = jnp.concatenate([before, shard, after], axis=dim)
    return shard


def along(vector, direction):
    total = jnp.zeros_like(vector[0])
    for axis_pos in range(3):
        if direction[axis_pos] == 1:
            total = total + vector[axis_pos]
        elif direction[axis_pos] == -1:
            total = total - vector[axis_pos]
    return total


def moments(fields):
    density = fields[0]
    for index in range(1, 19):
        density = density + fields[index]
    rows = []
    for axis_pos in range(3):
        total = jnp.zeros_like(density)
        for index in range(19):
            if VELOCITY[index][axis_pos] == 1:
                total = total + fields[index]
            elif VELOCITY[index][axis_pos] == -1:
                total = total - fields[index]
        rows.append(total)
    return (density, jnp.stack(rows))


def collide(fields, density, momentum, field):
    velocity = (momentum + 0.5 * field) / density
    square = velocity[0] * velocity[0] + velocity[1] * velocity[1] + velocity[2] * velocity[2]
    work = velocity[0] * field[0] + velocity[1] * field[1] + velocity[2] * field[2]
    outputs = []
    for index in range(19):
        proj_u = along(velocity, VELOCITY[index])
        proj_f = along(field, VELOCITY[index])
        equil = (
            WEIGHT[index] * density * (1.0 + 3.0 * proj_u + 4.5 * proj_u * proj_u - 1.5 * square)
        )
        source = (
            (1.0 - 0.5 / RELAX) * WEIGHT[index] * (3.0 * (proj_f - work) + 9.0 * proj_u * proj_f)
        )
        outputs.append(fields[index] - (fields[index] - equil) / RELAX + source)
    return jnp.stack(outputs)


def kernel_rows(position, span):
    count = position.shape[0]
    column = lax.broadcasted_iota(jnp.int32, (count, span), 1)
    total = jnp.zeros((count, span), jnp.float32)
    for shift_a in range(3):
        total = total + KERNEL[shift_a] * (column == position[:, None] + shift_a).astype(
            jnp.float32
        )
    return total


def on_device(populations, panels, modal_vel, marker_x, marker_y, marker_z, marker_riser):
    cells_x = populations.shape[1]
    cells_y = populations.shape[2]
    depth = populations.shape[3]
    widened = extended(populations, (("gx", 1), ("gy", 2)), 2)
    read_cycle = jnp.stack(
        [
            jnp.roll(
                widened[
                    i,
                    1 - VELOCITY[i][0] : 3 - VELOCITY[i][0] + cells_x,
                    1 - VELOCITY[i][1] : 3 - VELOCITY[i][1] + cells_y,
                ],
                VELOCITY[i][2],
                axis=2,
            )
            for i in range(19)
        ]
    )
    density_cycle, momentum_cycle = moments(read_cycle)
    fluid_cycle = momentum_cycle / density_cycle
    read = read_cycle[:, 1 : cells_x + 1, 1 : cells_y + 1]
    density = density_cycle[1 : cells_x + 1, 1 : cells_y + 1]
    momentum = momentum_cycle[:, 1 : cells_x + 1, 1 : cells_y + 1]
    targets = jnp.einsum(
        "rcm,rmz->rcz",
        modal_vel,
        lax.all_gather(panels, ("gx", "gy"), axis=2, tiled=True),
        preferred_element_type=jnp.float32,
    )
    pos_x = marker_x[0, 0]
    pos_y = marker_y[0, 0]
    pos_z = marker_z[0, 0]
    riser = marker_riser[0, 0]
    count = pos_x.shape[0]
    span_x = cells_x + 2
    span_y = cells_y + 2
    plane_size = span_x * span_y
    highest = lax.Precision.HIGHEST
    weight_x = kernel_rows(pos_x, span_x)
    weight_y = kernel_rows(pos_y, span_y)
    plane = (weight_x[:, :, None] * weight_y[:, None, :]).reshape(count, plane_size).T
    depth_hot = (lax.broadcasted_iota(jnp.int32, (count, depth), 1) == pos_z[:, None]).astype(
        jnp.float32
    )
    contract_depth = (((1,), (1,)), ((), ()))
    picked = lax.dot_general(
        fluid_cycle.reshape(3 * plane_size, depth),
        depth_hot,
        contract_depth,
        precision=highest,
        preferred_element_type=jnp.float32,
    )
    sampled = jnp.sum(picked.reshape(3, plane_size, count) * plane[None], axis=1)
    risers = targets.shape[0]
    target_cols = lax.dot_general(
        targets.reshape(risers * 2, depth),
        depth_hot,
        contract_depth,
        precision=highest,
        preferred_element_type=jnp.float32,
    ).reshape(risers, 2, count)
    riser_hot = (lax.broadcasted_iota(jnp.int32, (risers, count), 0) == riser[None, :]).astype(
        jnp.float32
    )
    chosen = jnp.sum(target_cols * riser_hot[:, None, :], axis=0)
    wanted = jnp.concatenate([chosen, jnp.zeros((1, count), jnp.float32)], axis=0)
    force = 2.0 * (wanted - sampled)
    spread = (force[:, None, :] * plane[None]).reshape(3 * plane_size, count)
    region = jnp.dot(
        spread, depth_hot, precision=highest, preferred_element_type=jnp.float32
    ).reshape(3, span_x, span_y, depth)
    rim_x = jnp.stack([region[:, 0], region[:, cells_x + 1]], axis=1)
    got_x = extended(rim_x, (("gx", 1),), 1)
    region = region.at[:, 1].add(got_x[:, 0]).at[:, cells_x].add(got_x[:, 3])
    inner = region[:, 1 : cells_x + 1]
    rim_y = jnp.stack([inner[:, :, 0], inner[:, :, cells_y + 1]], axis=2)
    got_y = extended(rim_y, (("gy", 2),), 1)
    inner = inner.at[:, :, 1].add(got_y[:, :, 0]).at[:, :, cells_y].add(got_y[:, :, 3])
    field = inner[:, :, 1 : cells_y + 1]
    next_populations = collide(read, density, momentum, field)
    return (next_populations, force[None, None], field)


def solution(mesh):
    in_specs = (
        P(None, "gx", "gy", None),
        P(None, None, ("gx", "gy")),
        P(),
        P("gx", "gy", None),
        P("gx", "gy", None),
        P("gx", "gy", None),
        P("gx", "gy", None),
    )
    out_specs = (P(None, "gx", "gy", None), P("gx", "gy", None, None), P(None, "gx", "gy", None))
    return jax.shard_map(
        on_device, mesh=mesh, in_specs=in_specs, out_specs=out_specs, check_vma=False
    )
```

profile of v0, /device:TPU:97, one launch (start us, length us, event | category | flops | bytes accessed | tf_op | source)
XLA Modules:
  0.0 365.4 jit_solution(12806877301452564051)
XLA Ops:
  7.2 1.8 fusion.221
  9.1 1.9 collective-permute-start
  14.9 2.1 constant_dynamic-update-slice_fusion.1
  16.9 4.3 %collective-permute-done.1 = f32[19,2,16,128]{3,2,1,0:T(8,128)} collective-permute-done((f32[19,2,16,128]{3,2,1,0:T(8,128)}, f32[19,2,16,128]{3,2,1,0:T(8,128)}, u32[]{:S(2)}, u32[]{:S(2)}) %collective-permute-start.1) | collective-permute-done | bytes 311328 | tf_op jit(solution)/shard_map/ppermute | solution.py:40
  23.5 2.8 collective-permute-start.3
  27.2 2.1 mul.602
  29.3 2.1 mul.608
  32.1 2.2 collective-permute-done.3
  34.3 4.3 %collective-permute-done.2 = f32[19,20,2,128]{3,2,1,0:T(2,128)} collective-permute-done((f32[19,20,2,128]{3,2,1,0:T(2,128)}, f32[19,20,2,128]{3,2,1,0:T(2,128)}, u32[]{:S(2)}, u32[]{:S(2)}) %collective-permute-start.2) | collective-permute-done | bytes 389152 | tf_op jit(solution)/shard_map/ppermute | solution.py:39
  38.6 2.0 maximum_bitcast_fusion.8
  42.1 1.9 concatenate.407
  44.8 2.1 slice_bitcast_fusion.21
  47.0 1.8 concatenate.411
  51.3 1.8 slice_reduce_fusion.9
  54.7 2.7 slice_reduce_fusion.5
  57.4 2.2 fusion.20
  64.8 2.0 add_subtract_fusion
  74.9 1.8 concatenate.413
  80.2 1.8 concatenate.418
  82.0 1.8 concatenate.421
  83.8 1.8 concatenate.419
  85.5 1.8 concatenate.424
  90.0 2.9 add_subtract_fusion.1
  92.9 1.8 stack.113
  96.4 3.8 %subtract_add_fusion = f32[1,18,18,128]{3,2,1,0:T(8,128)} fusion(f32[1,18,18,1]{3,2,1,0:T(8,128)} %copy-done.54, f32[1,18,18,127]{3,2,1,0:T(8,128)} %get-tuple-element.154, f32[1,18,18,127]{3,2,1,0:T(8,128)} %get-tuple-element.127, f32[1,18,18,1]{3,2,1,0:T(8,128)} %copy-done.52, f32[1,18,18,127]{3,2,1,0:T(8,128)} %copy-done.36, ...), kind=kLoop, calls=%fused_computation.72 | loop fusion | flops 787968 | bytes 1824768 | tf_op jit(solution)/shard_map/add | solution.py:64
  106.5 3.8 %fusion.27 = f32[1,324,128]{2,0,1:T(1,128)S(1)} fusion(f32[1,324,1]{2,0,1:T(1,128)S(1)} %copy-done.87, f32[1,324,127]{2,0,1:T(1,128)S(1)} %copy-done.85, f32[1,324,1]{2,0,1:T(1,128)S(1)} %copy-done.82, f32[1,324,127]{2,0,1:T(1,128)S(1)} %copy-done.84, f32[1,324,127]{2,0,1:T(1,128)S(1)} %copy-done.86, f32[1,324,1]{2,0,1:T(1,128)S(1)} %copy-done.88, ...), kind=kLoop, calls=%fused_computation.113 | loop fusion | flops 787968 | bytes 1824768 | tf_op jit(solution)/shard_map/add | solution.py:64
  112.5 204.5 %all-gather.2.cloned.1.call-done = bf16[64,200,128]{1,0,2:T(8,128)(2,1)} async-done(((bf16[64,200,1]{1,0,2:T(8,128)(2,1)}), bf16[64,200,128]{1,0,2:T(8,128)(2,1)}) %all-gather.2.cloned.1.call-update) | async-done | bytes 3276816 | tf_op jit(solution)/shard_map/all_gather | solution.py:127
  317.0 4.6 %fusion = f32[64,2,128]{2,1,0:T(2,128)S(1)} fusion(bf16[64,2,200]{2,1,0:T(2,128)(2,1)S(1)} %copy-done, bf16[64,200,128]{1,0,2:T(8,128)(2,1)} %all-gather.2.cloned.1.call-done), kind=kOutput, calls=%fused_computation | convolution fusion | flops 6553600 | bytes 3393536 | tf_op jit(solution)/shard_map/rcm,rmz->rcz/dot_general | solution.py:124
  323.7 2.7 collective-permute-start.4
  328.4 6.7 %collective-permute-done.5 = f32[3,1,18,128]{3,2,1,0:T(8,128)S(1)} collective-permute-done((f32[3,1,18,128]{3,2,1,0:T(8,128)S(1)}, f32[3,1,18,128]{3,2,1,0:T(8,128)S(1)}, u32[]{:S(2)}, u32[]{:S(2)}) %collective-permute-start.5) | collective-permute-done | bytes 27680 | tf_op jit(solution)/shard_map/ppermute | solution.py:40
  337.9 3.0 collective-permute-start.7
  345.3 2.3 fusion.9
  (307 shorter events, 65.0 us)
Async XLA Ops:
  7.2 309.9 %copy-start = (bf16[64,2,200]{2,1,0:T(2,128)(2,1)S(1)}, bf16[64,2,200]{2,1,0:T(2,128)(2,1)}, u32[]{:S(2)}) copy-start(bf16[64,2,200]{2,1,0:T(2,128)(2,1)} %param.17) | copy-start | bytes 153604
  7.2 309.8 %all-gather.2.cloned.1.call-start = ((), (), s32[]{:S(2)}) async-start(), calls=%async_computation | async-start | bytes 4227072 | tf_op jit(solution)/shard_map/all_gather | solution.py:127
  9.1 5.8 %collective-permute-start = (f32[19,2,16,128]{3,2,1,0:T(8,128)S(1)}, f32[19,2,16,128]{3,2,1,0:T(8,128)S(1)}, u32[]{:S(2)}, u32[]{:S(2)}) collective-permute-start(f32[19,2,16,128]{3,2,1,0:T(8,128)S(1)} %get-tuple-element.76), channel_id=1, source_target_pairs={{0,8},{8,16},{16,24},{24,32},{32,40},{40,48},{48,56},{56,64},{64,7... | collective-permute-start | bytes 933896 | tf_op jit(solution)/shard_map/ppermute | solution.py:39
  11.0 10.3 %collective-permute-start.1 = (f32[19,2,16,128]{3,2,1,0:T(8,128)}, f32[19,2,16,128]{3,2,1,0:T(8,128)}, u32[]{:S(2)}, u32[]{:S(2)}) collective-permute-start(f32[19,2,16,128]{3,2,1,0:T(8,128)} %get-tuple-element.75), channel_id=1, source_target_pairs={{8,0},{16,8},{24,16},{32,24},{40,32},{48,40},{56,48},{64,56},{72,6... | collective-permute-start | bytes 933896 | tf_op jit(solution)/shard_map/ppermute | solution.py:40
  22.2 9.2 %copy-start.108 = (s32[1,1,512]{2,1,0:T(1,128)S(1)}, s32[1,1,512]{2,1,0:T(1,128)}, u32[]{:S(2)}) copy-start(s32[1,1,512]{2,1,0:T(1,128)} %param.21) | copy-start | bytes 6148
  23.5 10.9 %collective-permute-start.3 = (f32[19,20,2,128]{3,2,1,0:T(2,128)}, f32[19,20,2,128]{3,2,1,0:T(2,128)}, u32[]{:S(2)}, u32[]{:S(2)}) collective-permute-start(f32[19,20,2,128]{3,2,1,0:T(2,128)} %get-tuple-element.74), channel_id=1, source_target_pairs={{1,0},{2,1},{3,2},{4,3},{5,4},{6,5},{7,6},{0,7},{9,8},{10,9},{11,1... | collective-permute-start | bytes 1167368 | tf_op jit(solution)/shard_map/ppermute | solution.py:40
  26.2 12.3 %collective-permute-start.2 = (f32[19,20,2,128]{3,2,1,0:T(2,128)}, f32[19,20,2,128]{3,2,1,0:T(2,128)}, u32[]{:S(2)}, u32[]{:S(2)}) collective-permute-start(f32[19,20,2,128]{3,2,1,0:T(2,128)} %get-tuple-element.73), channel_id=1, source_target_pairs={{0,1},{1,2},{2,3},{3,4},{4,5},{5,6},{6,7},{7,0},{8,9},{9,10},{10,1... | collective-permute-start | bytes 1167368 | tf_op jit(solution)/shard_map/ppermute | solution.py:39
  50.4 9.2 %copy-start.21 = (f32[18,18,127]{2,1,0:T(8,128)}, f32[18,18,127]{2,1,0:T(8,128)S(1)}, u32[]{:S(2)}) copy-start(f32[18,18,127]{2,1,0:T(8,128)S(1)} %get-tuple-element.128) | copy-start | bytes 493780
  53.1 14.6 %copy-start.52 = (f32[1,18,18,1]{3,2,1,0:T(8,128)}, f32[1,18,18,1]{3,2,1,0:T(8,128)S(1)}, u32[]{:S(2)}) copy-start(f32[1,18,18,1]{3,2,1,0:T(8,128)S(1)} %get-tuple-element.82) | copy-start | bytes 3892
  54.6 13.0 %copy-start.18 = (f32[1,18,18,1]{3,2,1,0:T(8,128)}, f32[1,18,18,1]{3,2,1,0:T(8,128)S(1)}, u32[]{:S(2)}) copy-start(f32[1,18,18,1]{3,2,1,0:T(8,128)S(1)} %get-tuple-element.88) | copy-start | bytes 3892
  54.6 13.0 %copy-start.54 = (f32[1,18,18,1]{3,2,1,0:T(8,128)}, f32[1,18,18,1]{3,2,1,0:T(8,128)S(1)}, u32[]{:S(2)}) copy-start(f32[1,18,18,1]{3,2,1,0:T(8,128)S(1)} %get-tuple-element.145) | copy-start | bytes 3892
  57.3 10.4 %copy-start.19 = (f32[1,18,18,1]{3,2,1,0:T(8,128)}, f32[1,18,18,1]{3,2,1,0:T(8,128)S(1)}, u32[]{:S(2)}) copy-start(f32[1,18,18,1]{3,2,1,0:T(8,128)S(1)} %get-tuple-element.94) | copy-start | bytes 3892
  57.3 10.4 %copy-start.20 = (f32[1,18,18,1]{3,2,1,0:T(8,128)}, f32[1,18,18,1]{3,2,1,0:T(8,128)S(1)}, u32[]{:S(2)}) copy-start(f32[1,18,18,1]{3,2,1,0:T(8,128)S(1)} %get-tuple-element.142) | copy-start | bytes 3892
  59.6 8.1 %copy-start.38 = (f32[1,18,18,128]{3,2,1,0:T(8,128)}, f32[1,18,18,128]{3,2,1,0:T(8,128)S(1)}, u32[]{:S(2)}) copy-start(f32[1,18,18,128]{3,2,1,0:T(8,128)S(1)} %get-tuple-element.58) | copy-start | bytes 497668
  59.6 8.1 %copy-start.39 = (f32[1,18,18,128]{3,2,1,0:T(8,128)}, f32[1,18,18,128]{3,2,1,0:T(8,128)S(1)}, u32[]{:S(2)}) copy-start(f32[1,18,18,128]{3,2,1,0:T(8,128)S(1)} %get-tuple-element.59) | copy-start | bytes 497668
  59.7 8.1 %copy-start.40 = (f32[1,18,18,128]{3,2,1,0:T(8,128)}, f32[1,18,18,128]{3,2,1,0:T(8,128)S(1)}, u32[]{:S(2)}) copy-start(f32[1,18,18,128]{3,2,1,0:T(8,128)S(1)} %get-tuple-element.60) | copy-start | bytes 497668
  59.7 8.1 %copy-start.41 = (f32[1,18,18,128]{3,2,1,0:T(8,128)}, f32[1,18,18,128]{3,2,1,0:T(8,128)S(1)}, u32[]{:S(2)}) copy-start(f32[1,18,18,128]{3,2,1,0:T(8,128)S(1)} %get-tuple-element.61) | copy-start | bytes 497668
  68.4 8.3 %copy-start.104 = (f32[18,18]{1,0:T(8,128)S(1)}, f32[18,18]{1,0:T(8,128)}, u32[]{:S(2)}) copy-start(f32[18,18]{1,0:T(8,128)} %get-tuple-element.143) | copy-start | bytes 3892
  68.4 9.2 %copy-start.103 = (f32[18,18]{1,0:T(8,128)S(1)}, f32[18,18]{1,0:T(8,128)}, u32[]{:S(2)}) copy-start(f32[18,18]{1,0:T(8,128)} %get-tuple-element.93) | copy-start | bytes 3892
  69.8 19.3 %copy-start.105 = (f32[18,18]{1,0:T(8,128)S(1)}, f32[18,18]{1,0:T(8,128)}, u32[]{:S(2)}) copy-start(f32[18,18]{1,0:T(8,128)} %get-tuple-element.81) | copy-start | bytes 3892
  96.4 7.4 %copy-start.5 = (f32[18,18,127]{2,1,0:T(8,128)S(1)}, f32[18,18,127]{2,1,0:T(8,128)}, u32[]{:S(2)}) copy-start(f32[18,18,127]{2,1,0:T(8,128)} %get-tuple-element.116) | copy-start | bytes 493780
  96.4 7.4 %copy-start.47 = (f32[18,18,1]{2,1,0:T(8,128)S(1)}, f32[18,18,1]{2,1,0:T(8,128)}, u32[]{:S(2)}) copy-start(f32[18,18,1]{2,1,0:T(8,128)} %get-tuple-element.95) | copy-start | bytes 3892
  112.5 215.0 %copy-start.9 = (f32[18,18,127]{2,1,0:T(8,128)S(1)}, f32[18,18,127]{2,1,0:T(8,128)}, u32[]{:S(2)}) copy-start(f32[18,18,127]{2,1,0:T(8,128)} %get-tuple-element.124) | copy-start | bytes 493780
  317.0 9.3 %copy-start.11 = (f32[18,18,127]{2,1,0:T(8,128)S(1)}, f32[18,18,127]{2,1,0:T(8,128)}, u32[]{:S(2)}) copy-start(f32[18,18,127]{2,1,0:T(8,128)} %get-tuple-element.147) | copy-start | bytes 493780
  317.0 9.3 %copy-start.49 = (f32[18,18,1]{2,1,0:T(8,128)S(1)}, f32[18,18,1]{2,1,0:T(8,128)}, u32[]{:S(2)}) copy-start(f32[18,18,1]{2,1,0:T(8,128)} %get-tuple-element.135) | copy-start | bytes 3892
  317.0 10.5 %copy-start.46 = (f32[18,18,1]{2,1,0:T(8,128)S(1)}, f32[18,18,1]{2,1,0:T(8,128)}, u32[]{:S(2)}) copy-start(f32[18,18,1]{2,1,0:T(8,128)} %get-tuple-element.107) | copy-start | bytes 3892
  321.7 14.6 %copy-start.7 = (f32[18,18,127]{2,1,0:T(8,128)S(1)}, f32[18,18,127]{2,1,0:T(8,128)}, u32[]{:S(2)}) copy-start(f32[18,18,127]{2,1,0:T(8,128)} %get-tuple-element.126) | copy-start | bytes 493780
  321.7 14.6 %copy-start.44 = (f32[18,18,1]{2,1,0:T(8,128)S(1)}, f32[18,18,1]{2,1,0:T(8,128)}, u32[]{:S(2)}) copy-start(f32[18,18,1]{2,1,0:T(8,128)} %get-tuple-element.104) | copy-start | bytes 3892
  323.7 3.8 %collective-permute-start.4 = (f32[3,1,18,128]{3,2,1,0:T(8,128)S(1)}, f32[3,1,18,128]{3,2,1,0:T(8,128)S(1)}, u32[]{:S(2)}, u32[]{:S(2)}) collective-permute-start(f32[3,1,18,128]{3,2,1,0:T(8,128)S(1)} %slice.611), channel_id=1, source_target_pairs={{0,8},{8,16},{16,24},{24,32},{32,40},{40,48},{48,56},{56,64},{64,7... | collective-permute-start | bytes 82952 | tf_op jit(solution)/shard_map/ppermute | solution.py:39
  327.4 7.6 %collective-permute-start.5 = (f32[3,1,18,128]{3,2,1,0:T(8,128)S(1)}, f32[3,1,18,128]{3,2,1,0:T(8,128)S(1)}, u32[]{:S(2)}, u32[]{:S(2)}) collective-permute-start(f32[3,1,18,128]{3,2,1,0:T(8,128)S(1)} %get-tuple-element.79), channel_id=1, source_target_pairs={{8,0},{16,8},{24,16},{32,24},{40,32},{48,40},{56,48},{64,56},{72,6... | collective-permute-start | bytes 82952 | tf_op jit(solution)/shard_map/ppermute | solution.py:40
  335.7 5.2 %collective-permute-start.6 = (f32[3,16,1,128]{3,2,1,0:T(1,128)S(1)}, f32[3,16,1,128]{3,2,1,0:T(1,128)S(1)}, u32[]{:S(2)}, u32[]{:S(2)}) collective-permute-start(f32[3,16,1,128]{3,2,1,0:T(1,128)S(1)} %get-tuple-element.78), channel_id=1, source_target_pairs={{0,1},{1,2},{2,3},{3,4},{4,5},{5,6},{6,7},{7,0},{8,9},{9,10},{10,1... | collective-permute-start | bytes 73736 | tf_op jit(solution)/shard_map/ppermute | solution.py:39
  337.9 4.8 %collective-permute-start.7 = (f32[3,16,1,128]{3,2,1,0:T(1,128)}, f32[3,16,1,128]{3,2,1,0:T(1,128)}, u32[]{:S(2)}, u32[]{:S(2)}) collective-permute-start(f32[3,16,1,128]{3,2,1,0:T(1,128)} %get-tuple-element.77), channel_id=1, source_target_pairs={{1,0},{2,1},{3,2},{4,3},{5,4},{6,5},{7,6},{0,7},{9,8},{10,9},{11,1... | collective-permute-start | bytes 73736 | tf_op jit(solution)/shard_map/ppermute | solution.py:40
  (86 other events, 371.3 us)
Sparse Core Ops, SparseCore 0:
  11.1 305.8 all-gather.1
where the time goes:
time: 367 us; the launch traced here: 365 us
  waiting for transfers between devices  224 us (61%)
  local copies, waits for them, and re-layouts  64 us (17%)
  other arithmetic  43.4 us (12%)
  between operations  15.3 us (4%)
  starting transfers between devices  11.1 us (3%)
  matrix products  7.67 us (2%)
    all_gather x1, waiting for transfers between devices, on_device(): lax.all_gather(panels, ('gx', 'gy'), axis=2, tiled=True)  205 us
    concatenate x26, local copies, waits for them, and re-layouts, on_device(): jnp.roll(widened[i, 1 - VELOCITY[i][0]:3 - VELOCITY[i][0] + cells_x, 1 -...  30.5 us
    ppermute x4, waiting for transfers between devices, extended(): after = lax.ppermute(first, axis, down)  13.2 us
    slice x6, local copies, waits for them, and re-layouts, on_device(): jnp.roll(widened[i, 1 - VELOCITY[i][0]:3 - VELOCITY[i][0] + cells_x, 1 -...  8.64 us
    unnamed x18, other arithmetic  8.58 us
    add x2, other arithmetic, moments(): total = total + fields[index]  7.64 us
    another operation x10, other arithmetic, on_device(): jnp.stack([jnp.roll(widened[i, 1 - VELOCITY[i][0]:3 - VELOCITY[i][0] + ce...  7.54 us
  transfers between devices with their start and end apart: 9, of which 7 were waited for; matrix products, arithmetic and copies ran while one was open for 24% of the time, Pallas kernels for 0%

commit v1 on v0

--- a/solution.py
+++ b/solution.py
@@ -98,6 +98,13 @@
 
 
 def on_device(populations, panels, modal_vel, marker_x, marker_y, marker_z, marker_riser):
+
+    def end_row_in(chunk, array_dim=2):
+        piece_next = jax.lax.axis_size(("gx", "gy"))
+        p_next = jnp.stack([chunk] * piece_next)
+        z = jax.lax.all_to_all(p_next, axis_name=("gx", "gy"), split_axis=0, concat_axis=0)
+        return jnp.concatenate(z, axis=array_dim)
+
     cells_x = populations.shape[1]
     cells_y = populations.shape[2]
     depth = populations.shape[3]
@@ -122,10 +129,7 @@
     density = density_cycle[1 : cells_x + 1, 1 : cells_y + 1]
     momentum = momentum_cycle[:, 1 : cells_x + 1, 1 : cells_y + 1]
     targets = jnp.einsum(
-        "rcm,rmz->rcz",
-        modal_vel,
-        lax.all_gather(panels, ("gx", "gy"), axis=2, tiled=True),
-        preferred_element_type=jnp.float32,
+        "rcm,rmz->rcz", modal_vel, end_row_in(panels), preferred_element_type=jnp.float32
     )
     pos_x = marker_x[0, 0]
     pos_y = marker_y[0, 0]

time: 367 us -> 198 us (0.54)
  waiting for transfers between devices: 224 us -> 49.8 us
  between operations: 15.3 us -> 1.86 us
  starting transfers between devices: 11.1 us -> 23 us
  local copies, waits for them, and re-layouts: 64 us -> 73.5 us
    all_gather x1 -> x0, waiting for transfers between devices: 205 us -> none  [on_device(): lax.all_gather(panels, ('gx', 'gy'), axis=2, tiled=True)]
    ppermute x4, waiting for transfers between devices: 13.2 us -> 49.6 us  [extended(): after = lax.ppermute(first, axis, down)]
    all_to_all x0 -> x1, starting transfers between devices: none -> 10.5 us  [end_row_in(): jax.lax.all_to_all(p_next, axis_name=('gx', 'gy'), split_axis=0, concat_a...]
    all_to_all x0 -> x1, local copies, waits for them, and re-layouts: none -> 6.7 us  [end_row_in(): jax.lax.all_to_all(p_next, axis_name=('gx', 'gy'), split_axis=0, concat_a...]
    ppermute x4, waiting for transfers between devices: 6.17 us -> 0.26 us  [extended(): before = lax.ppermute(last, axis, up)]
  transfers between devices with their start and end apart: 9 -> 9, of which waited for: 7 -> 3; matrix products, arithmetic and copies ran while one was open for 24% -> 47% of each run, Pallas kernels for 0% -> 0%
where the time goes in v1:
time: 198 us; the launch traced here: 196 us
  local copies, waits for them, and re-layouts  73.5 us (37%)
  waiting for transfers between devices  49.8 us (25%)
  other arithmetic  41.8 us (21%)
  starting transfers between devices  23 us (12%)
  matrix products  6.07 us (3%)
    ppermute x4, waiting for transfers between devices, extended(): after = lax.ppermute(first, axis, down)  49.6 us
    concatenate x26, local copies, waits for them, and re-layouts, on_device(): jnp.roll(widened[i, 1 - VELOCITY[i][0]:3 - VELOCITY[i][0] + cells_x, 1 -...  30.2 us
    all_to_all x1, starting transfers between devices, end_row_in(): jax.lax.all_to_all(p_next, axis_name=('gx', 'gy'), split_axis=0, concat_a...  10.5 us
    another operation x10, other arithmetic, on_device(): jnp.stack([jnp.roll(widened[i, 1 - VELOCITY[i][0]:3 - VELOCITY[i][0] + ce...  8.12 us
    slice x6, local copies, waits for them, and re-layouts, on_device(): jnp.roll(widened[i, 1 - VELOCITY[i][0]:3 - VELOCITY[i][0] + cells_x, 1 -...  8.09 us
    add x2, other arithmetic, moments(): total = total + fields[index]  7.66 us
    add x3, other arithmetic, moments(): density = density + fields[index]  7.27 us
    ppermute x4, starting transfers between devices, extended(): after = lax.ppermute(first, axis, down)  7.16 us
  transfers between devices with their start and end apart: 9, of which 3 were waited for; matrix products, arithmetic and copies ran while one was open for 47% of the time, Pallas kernels for 0%

profile of v1, /device:TPU:97, one launch (start us, length us, event | category | flops | bytes accessed | tf_op | source)
XLA Modules:
  0.0 196.1 jit_solution(6225741025769865404)
XLA Ops:
  0.6 1.9 fusion.221
  2.5 1.9 collective-permute-start
  4.4 3.3 %stack.71 = bf16[128,64,200,1]{2,1,3,0:T(8,128)(2,1)} broadcast(bf16[64,200]{1,0:T(8,128)(2,1)} %bitcast.445), dimensions={1,2} | broadcast | bytes 3302400 | tf_op jit(solution)/shard_map/stack | solution.py:104
  7.8 10.5 %all-to-all-start = ((bf16[128,64,200,1]{2,1,3,0:T(8,128)(2,1)}), bf16[128,64,200,1]{2,1,3,0:T(8,128)(2,1)}, u32[]{:S(2)}, u32[]{:S(2)}) async-start(bf16[128,64,200,1]{2,1,3,0:T(8,128)(2,1)} %stack.71), calls=%async_computation | async-start | bytes 8388608 | tf_op jit(solution)/shard_map/all_to_all | solution.py:105
  18.5 2.0 %constant_dynamic-update-slice_fusion.1 = f32[19,20,16,128]{3,2,1,0:T(8,128)S(1)} fusion(f32[19,20,16,128]{3,2,1,0:T(8,128)S(1)} %constant_dynamic-update-slice_fusion.2, f32[19,16,16,128]{3,2,1,0:T(8,128)} %param.15), kind=kLoop, calls=%fused_computation.343 | loop fusion | bytes 4980736
  22.7 3.5 %collective-permute-start.3 = (f32[19,20,2,128]{3,2,1,0:T(2,128)}, f32[19,20,2,128]{3,2,1,0:T(2,128)}, u32[]{:S(2)}, u32[]{:S(2)}) collective-permute-start(f32[19,20,2,128]{3,2,1,0:T(2,128)} %get-tuple-element.74), channel_id=1, source_target_pairs={{1,0},{2,1},{3,2},{4,3},{5,4},{6,5},{7,6},{0,7},{9,8},{10,9},{11,1... | collective-permute-start | bytes 1167368 | tf_op jit(solution)/shard_map/ppermute | solution.py:40
  27.2 2.1 %mul.602 = f32[512,324]{0,1:T(8,128)} reshape(f32[512,18,18]{0,2,1:T(8,128)} %broadcast_multiply_fusion) | data formatting | bytes 1327104 | tf_op jit(solution)/shard_map/mul | solution.py:145
  29.3 2.1 %mul.608 = f32[18,18,512]{2,1,0:T(8,128)} reshape(f32[324,512]{1,0:T(8,128)} %bitcast.443) | data formatting | bytes 1327104 | tf_op jit(solution)/shard_map/mul | solution.py:157
  32.0 42.8 %collective-permute-done.3 = f32[19,20,2,128]{3,2,1,0:T(2,128)} collective-permute-done((f32[19,20,2,128]{3,2,1,0:T(2,128)}, f32[19,20,2,128]{3,2,1,0:T(2,128)}, u32[]{:S(2)}, u32[]{:S(2)}) %collective-permute-start.3) | collective-permute-done | bytes 389152 | tf_op jit(solution)/shard_map/ppermute | solution.py:40
  88.8 1.8 concatenate.419
  91.4 1.8 concatenate.421
  94.9 1.8 concatenate.418
  97.6 1.8 concatenate.411
  99.3 1.8 concatenate.410
  101.1 1.8 concatenate.407
  102.8 1.8 concatenate.406
  104.7 2.9 %fusion.20 = (f32[18,18,128]{2,1,0:T(8,128)}, f32[1,18,18,128]{3,2,1,0:T(8,128)}, f32[1,18,18,128]{3,2,1,0:T(8,128)S(1)}, f32[1,18,18,128]{3,2,1,0:T(8,128)S(1)}...) fusion(f32[18,18,1]{2,1,0:T(8,128)} %get-tuple-element.141, f32[18,18,127]{2,1,0:T(8,128)} %get-tuple-element.151, ...), kind=kLoop, calls=%fused_computation.65 | loop fusion | flops 1161216 | bytes 5550080 | tf_op jit(solution)/shard_map/add | solution.py:58
  107.7 1.9 add_subtract_fusion
  111.9 1.8 slice_reduce_fusion.4
  115.5 1.8 concatenate.413
  120.8 1.8 stack.73
  122.6 2.8 %add_subtract_fusion.1 = f32[1,18,18,128]{3,2,1,0:T(8,128)} fusion(f32[1,18,18,128]{3,2,1,0:T(8,128)} %copy-done.32, f32[1,18,18,128]{3,2,1,0:T(8,128)} %copy-done.31, f32[1,18,18,128]{3,2,1,0:T(8,128)} %copy-done.30, f32[1,18,18,128]{3,2,1,0:T(8,128)} %copy-done.29, f32[19,20,2,128]{3,2,1,0:T(2,128)} %collective-permute-done.3, ...), kind=kLoop, calls=%fused_computation.74 | loop fusion | flops 705024 | bytes 5384192 | tf_op jit(solution)/shard_map/sub | solution.py:66
  125.5 1.8 stack.72
  127.2 4.0 %add_add_fusion = f32[1,18,18,128]{3,2,1,0:T(8,128)} fusion(f32[1,18,18,128]{3,2,1,0:T(8,128)} %copy-done.32, f32[1,18,18,128]{3,2,1,0:T(8,128)} %copy-done.31, f32[1,18,18,128]{3,2,1,0:T(8,128)} %copy-done.30, f32[1,18,18,128]{3,2,1,0:T(8,128)} %copy-done.29, f32[1,18,18,128]{3,2,1,0:T(8,128)} %get-tuple-element.57, ...), kind=kLoop, calls=%fused_computation.71 | loop fusion | flops 995328 | bytes 2654208 | tf_op jit(solution)/shard_map/add | solution.py:58
  133.0 3.8 %subtract_add_fusion = f32[1,18,18,128]{3,2,1,0:T(8,128)} fusion(f32[1,18,18,1]{3,2,1,0:T(8,128)} %get-tuple-element.145, f32[1,18,18,127]{3,2,1,0:T(8,128)} %get-tuple-element.154, f32[1,18,18,127]{3,2,1,0:T(8,128)} %get-tuple-element.127, f32[1,18,18,1]{3,2,1,0:T(8,128)} %get-tuple-element.82, f32[1,18,18,127]{3,2,1,0:T(8,128)} %get-tuple-element.125, ...), kind=kLoop, calls=%fused_computation.72 | loop fusion | flops 787968 | bytes 1824768 | tf_op jit(solution)/shard_map/add | solution.py:64
  143.0 3.8 %fusion.27 = f32[1,324,128]{2,0,1:T(1,128)S(1)} fusion(f32[1,324,1]{2,0,1:T(1,128)S(1)} %copy-done.51, f32[1,324,127]{2,0,1:T(1,128)S(1)} %copy-done.52, f32[1,324,1]{2,0,1:T(1,128)S(1)} %copy-done.53, f32[1,324,127]{2,0,1:T(1,128)S(1)} %copy-done.54, f32[1,324,127]{2,0,1:T(1,128)S(1)} %copy-done.55, f32[1,324,1]{2,0,1:T(1,128)S(1)} %copy-done.56, ...), kind=kLoop, calls=%fused_computation.113 | loop fusion | flops 787968 | bytes 1824768 | tf_op jit(solution)/shard_map/add | solution.py:64
  149.0 6.7 %copy.75 = bf16[128,64,200,1]{0,2,1,3:T(8,128)(2,1)} copy(bf16[128,64,200,1]{2,1,3,0:T(8,128)(2,1)} %all-to-all-done) | data formatting | bytes 6553600 | tf_op jit(solution)/shard_map/all_to_all | solution.py:105
  155.7 3.0 %fusion = f32[64,2,128]{2,1,0:T(2,128)S(1)} fusion(bf16[64,2,200]{2,1,0:T(2,128)(2,1)S(1)} %copy-done, bf16[128,64,200,1]{0,2,1,3:T(8,128)(2,1)} %copy.75), kind=kOutput, calls=%fused_computation | convolution fusion | flops 6553600 | bytes 3393536 | tf_op jit(solution)/shard_map/rcm,rmz->rcz/dot_general | solution.py:131
  160.8 3.4 %collective-permute-start.4 = (f32[3,1,18,128]{3,2,1,0:T(8,128)S(1)}, f32[3,1,18,128]{3,2,1,0:T(8,128)S(1)}, u32[]{:S(2)}, u32[]{:S(2)}) collective-permute-start(f32[3,1,18,128]{3,2,1,0:T(8,128)S(1)} %slice.611), channel_id=1, source_target_pairs={{0,8},{8,16},{16,24},{24,32},{32,40},{40,48},{48,56},{56,64},{64,7... | collective-permute-start | bytes 82952 | tf_op jit(solution)/shard_map/ppermute | solution.py:39
  166.1 6.7 %collective-permute-done.5 = f32[3,1,18,128]{3,2,1,0:T(8,128)S(1)} collective-permute-done((f32[3,1,18,128]{3,2,1,0:T(8,128)S(1)}, f32[3,1,18,128]{3,2,1,0:T(8,128)S(1)}, u32[]{:S(2)}, u32[]{:S(2)}) %collective-permute-start.5) | collective-permute-done | bytes 27680 | tf_op jit(solution)/shard_map/ppermute | solution.py:40
  175.8 3.6 %collective-permute-start.7 = (f32[3,16,1,128]{3,2,1,0:T(1,128)}, f32[3,16,1,128]{3,2,1,0:T(1,128)}, u32[]{:S(2)}, u32[]{:S(2)}) collective-permute-start(f32[3,16,1,128]{3,2,1,0:T(1,128)} %get-tuple-element.77), channel_id=1, source_target_pairs={{1,0},{2,1},{3,2},{4,3},{5,4},{6,5},{7,6},{0,7},{9,8},{10,9},{11,1... | collective-permute-start | bytes 73736 | tf_op jit(solution)/shard_map/ppermute | solution.py:40
  183.7 2.3 %fusion.9 = (f32[3,16,16,128]{3,2,1,0:T(8,128)S(1)}, f32[3,16,16,128]{3,2,1,0:T(8,128)}) fusion(f32[1,18,18,128]{3,2,1,0:T(8,128)} %subtract_add_fusion, f32[1,18,18,128]{3,2,1,0:T(8,128)} %get-tuple-element.62, f32[1,18,18,128]{3,2,1,0:T(8,128)S(1)} %copy-done.42, f32[16,16,128]{2,1,0:T(8,128)S(1)} %fusion.191, f32[3,16,18,128]{3,2,1,0:T(8,128)} %scatter-add.19), kind=kLoop, calls=%fused_computation.14 | loop fusion | flops 491520 | bytes 1808384 | tf_op jit(solution)/shard_map/div | solution.py:72
  (276 shorter events, 59.5 us)
Async XLA Ops:
  0.6 155.0 %copy-start = (bf16[64,2,200]{2,1,0:T(2,128)(2,1)S(1)}, bf16[64,2,200]{2,1,0:T(2,128)(2,1)}, u32[]{:S(2)}) copy-start(bf16[64,2,200]{2,1,0:T(2,128)(2,1)} %param.17) | copy-start | bytes 153604
  2.5 15.9 %collective-permute-start = (f32[19,2,16,128]{3,2,1,0:T(8,128)S(1)}, f32[19,2,16,128]{3,2,1,0:T(8,128)S(1)}, u32[]{:S(2)}, u32[]{:S(2)}) collective-permute-start(f32[19,2,16,128]{3,2,1,0:T(8,128)S(1)} %get-tuple-element.76), channel_id=1, source_target_pairs={{0,8},{8,16},{16,24},{24,32},{32,40},{40,48},{48,56},{56,64},{64,7... | collective-permute-start | bytes 933896 | tf_op jit(solution)/shard_map/ppermute | solution.py:39
  4.4 16.1 %collective-permute-start.1 = (f32[19,2,16,128]{3,2,1,0:T(8,128)}, f32[19,2,16,128]{3,2,1,0:T(8,128)}, u32[]{:S(2)}, u32[]{:S(2)}) collective-permute-start(f32[19,2,16,128]{3,2,1,0:T(8,128)} %get-tuple-element.75), channel_id=1, source_target_pairs={{8,0},{16,8},{24,16},{32,24},{40,32},{48,40},{56,48},{64,56},{72,6... | collective-permute-start | bytes 933896 | tf_op jit(solution)/shard_map/ppermute | solution.py:40
  7.8 10.6 %copy-start.89 = (s32[1,1,512]{2,1,0:T(1,128)S(1)}, s32[1,1,512]{2,1,0:T(1,128)}, u32[]{:S(2)}) copy-start(s32[1,1,512]{2,1,0:T(1,128)} %param.19) | copy-start | bytes 6148
  7.8 10.6 %copy-start.90 = (s32[1,1,512]{2,1,0:T(1,128)S(1)}, s32[1,1,512]{2,1,0:T(1,128)}, u32[]{:S(2)}) copy-start(s32[1,1,512]{2,1,0:T(1,128)} %param.18) | copy-start | bytes 6148
  7.8 141.2 %all-to-all-start = ((bf16[128,64,200,1]{2,1,3,0:T(8,128)(2,1)}), bf16[128,64,200,1]{2,1,3,0:T(8,128)(2,1)}, u32[]{:S(2)}, u32[]{:S(2)}) async-start(bf16[128,64,200,1]{2,1,3,0:T(8,128)(2,1)} %stack.71), calls=%async_computation | async-start | bytes 8388608 | tf_op jit(solution)/shard_map/all_to_all | solution.py:105
  21.5 9.9 %copy-start.92 = (s32[1,1,512]{2,1,0:T(1,128)S(1)}, s32[1,1,512]{2,1,0:T(1,128)}, u32[]{:S(2)}) copy-start(s32[1,1,512]{2,1,0:T(1,128)} %param.21) | copy-start | bytes 6148
  22.7 52.2 %collective-permute-start.3 = (f32[19,20,2,128]{3,2,1,0:T(2,128)}, f32[19,20,2,128]{3,2,1,0:T(2,128)}, u32[]{:S(2)}, u32[]{:S(2)}) collective-permute-start(f32[19,20,2,128]{3,2,1,0:T(2,128)} %get-tuple-element.74), channel_id=1, source_target_pairs={{1,0},{2,1},{3,2},{4,3},{5,4},{6,5},{7,6},{0,7},{9,8},{10,9},{11,1... | collective-permute-start | bytes 1167368 | tf_op jit(solution)/shard_map/ppermute | solution.py:40
  32.0 45.5 %collective-permute-start.2 = (f32[19,20,2,128]{3,2,1,0:T(2,128)}, f32[19,20,2,128]{3,2,1,0:T(2,128)S(1)}, u32[]{:S(2)}, u32[]{:S(2)}) collective-permute-start(f32[19,20,2,128]{3,2,1,0:T(2,128)} %get-tuple-element.73), channel_id=1, source_target_pairs={{0,1},{1,2},{2,3},{3,4},{4,5},{5,6},{6,7},{7,0},{8,9},{9,10},{10,1... | collective-permute-start | bytes 1167368 | tf_op jit(solution)/shard_map/ppermute | solution.py:39
  77.6 15.6 %copy-start.8 = (f32[18,18,127]{2,1,0:T(8,128)}, f32[18,18,127]{2,1,0:T(8,128)S(1)}, u32[]{:S(2)}) copy-start(f32[18,18,127]{2,1,0:T(8,128)S(1)} %get-tuple-element.126) | copy-start | bytes 493780
  109.6 8.5 %copy-start.86 = (f32[18,18]{1,0:T(8,128)S(1)}, f32[18,18]{1,0:T(8,128)}, u32[]{:S(2)}) copy-start(f32[18,18]{1,0:T(8,128)} %get-tuple-element.87) | copy-start | bytes 3892
  109.6 9.4 %copy-start.85 = (f32[18,18]{1,0:T(8,128)S(1)}, f32[18,18]{1,0:T(8,128)}, u32[]{:S(2)}) copy-start(f32[18,18]{1,0:T(8,128)} %get-tuple-element.146) | copy-start | bytes 3892
  109.7 10.3 %copy-start.87 = (f32[18,18]{1,0:T(8,128)S(1)}, f32[18,18]{1,0:T(8,128)}, u32[]{:S(2)}) copy-start(f32[18,18]{1,0:T(8,128)} %get-tuple-element.81) | copy-start | bytes 3892
  132.9 6.6 %copy-start.18 = (f32[18,18,127]{2,1,0:T(8,128)S(1)}, f32[18,18,127]{2,1,0:T(8,128)}, u32[]{:S(2)}) copy-start(f32[18,18,127]{2,1,0:T(8,128)} %get-tuple-element.151) | copy-start | bytes 493780
  132.9 6.5 %copy-start.45 = (f32[18,18,1]{2,1,0:T(8,128)S(1)}, f32[18,18,1]{2,1,0:T(8,128)}, u32[]{:S(2)}) copy-start(f32[18,18,1]{2,1,0:T(8,128)} %get-tuple-element.141) | copy-start | bytes 3892
  132.9 7.3 %copy-start.16 = (f32[18,18,127]{2,1,0:T(8,128)S(1)}, f32[18,18,127]{2,1,0:T(8,128)}, u32[]{:S(2)}) copy-start(f32[18,18,127]{2,1,0:T(8,128)} %get-tuple-element.116) | copy-start | bytes 493780
  132.9 7.3 %copy-start.41 = (f32[18,18,1]{2,1,0:T(8,128)S(1)}, f32[18,18,1]{2,1,0:T(8,128)}, u32[]{:S(2)}) copy-start(f32[18,18,1]{2,1,0:T(8,128)} %get-tuple-element.95) | copy-start | bytes 3892
  136.8 5.9 %copy-start.51 = (f32[1,324,1]{2,0,1:T(1,128)S(1)}, f32[1,324,1]{2,0,1:T(1,128)}, u32[]{:S(2)}) copy-start(f32[1,324,1]{2,0,1:T(1,128)} %concatenate.420) | copy-start | bytes 3892
  136.8 5.9 %copy-start.52 = (f32[1,324,127]{2,0,1:T(1,128)S(1)}, f32[1,324,127]{2,0,1:T(1,128)}, u32[]{:S(2)}) copy-start(f32[1,324,127]{2,0,1:T(1,128)} %concatenate.419) | copy-start | bytes 493780
  136.8 5.9 %copy-start.53 = (f32[1,324,1]{2,0,1:T(1,128)S(1)}, f32[1,324,1]{2,0,1:T(1,128)}, u32[]{:S(2)}) copy-start(f32[1,324,1]{2,0,1:T(1,128)} %concatenate.422) | copy-start | bytes 3892
  136.9 5.9 %copy-start.54 = (f32[1,324,127]{2,0,1:T(1,128)S(1)}, f32[1,324,127]{2,0,1:T(1,128)}, u32[]{:S(2)}) copy-start(f32[1,324,127]{2,0,1:T(1,128)} %concatenate.421) | copy-start | bytes 493780
  155.7 8.4 %copy-start.12 = (f32[18,18,127]{2,1,0:T(8,128)S(1)}, f32[18,18,127]{2,1,0:T(8,128)}, u32[]{:S(2)}) copy-start(f32[18,18,127]{2,1,0:T(8,128)} %get-tuple-element.147) | copy-start | bytes 493780
  155.7 8.4 %copy-start.37 = (f32[18,18,1]{2,1,0:T(8,128)S(1)}, f32[18,18,1]{2,1,0:T(8,128)}, u32[]{:S(2)}) copy-start(f32[18,18,1]{2,1,0:T(8,128)} %get-tuple-element.135) | copy-start | bytes 3892
  155.7 9.6 %copy-start.14 = (f32[18,18,127]{2,1,0:T(8,128)S(1)}, f32[18,18,127]{2,1,0:T(8,128)}, u32[]{:S(2)}) copy-start(f32[18,18,127]{2,1,0:T(8,128)} %get-tuple-element.124) | copy-start | bytes 493780
  155.7 9.6 %copy-start.39 = (f32[18,18,1]{2,1,0:T(8,128)S(1)}, f32[18,18,1]{2,1,0:T(8,128)}, u32[]{:S(2)}) copy-start(f32[18,18,1]{2,1,0:T(8,128)} %get-tuple-element.107) | copy-start | bytes 3892
  158.8 14.7 %copy-start.10 = (f32[18,18,127]{2,1,0:T(8,128)S(1)}, f32[18,18,127]{2,1,0:T(8,128)}, u32[]{:S(2)}) copy-start(f32[18,18,127]{2,1,0:T(8,128)} %copy-done.8) | copy-start | bytes 493780
  158.8 14.7 %copy-start.35 = (f32[18,18,1]{2,1,0:T(8,128)S(1)}, f32[18,18,1]{2,1,0:T(8,128)}, u32[]{:S(2)}) copy-start(f32[18,18,1]{2,1,0:T(8,128)} %get-tuple-element.104) | copy-start | bytes 3892
  159.2 24.5 %copy-start.42 = (f32[1,18,18,128]{3,2,1,0:T(8,128)S(1)}, f32[1,18,18,128]{3,2,1,0:T(8,128)}, u32[]{:S(2)}) copy-start(f32[1,18,18,128]{3,2,1,0:T(8,128)} %add_subtract_fusion.1) | copy-start | bytes 497668
  160.8 4.4 %collective-permute-start.4 = (f32[3,1,18,128]{3,2,1,0:T(8,128)S(1)}, f32[3,1,18,128]{3,2,1,0:T(8,128)S(1)}, u32[]{:S(2)}, u32[]{:S(2)}) collective-permute-start(f32[3,1,18,128]{3,2,1,0:T(8,128)S(1)} %slice.611), channel_id=1, source_target_pairs={{0,8},{8,16},{16,24},{24,32},{32,40},{40,48},{48,56},{56,64},{64,7... | collective-permute-start | bytes 82952 | tf_op jit(solution)/shard_map/ppermute | solution.py:39
  165.2 7.6 %collective-permute-start.5 = (f32[3,1,18,128]{3,2,1,0:T(8,128)S(1)}, f32[3,1,18,128]{3,2,1,0:T(8,128)S(1)}, u32[]{:S(2)}, u32[]{:S(2)}) collective-permute-start(f32[3,1,18,128]{3,2,1,0:T(8,128)S(1)} %get-tuple-element.79), channel_id=1, source_target_pairs={{8,0},{16,8},{24,16},{32,24},{40,32},{48,40},{56,48},{64,56},{72,6... | collective-permute-start | bytes 82952 | tf_op jit(solution)/shard_map/ppermute | solution.py:40
  173.5 5.8 %collective-permute-start.6 = (f32[3,16,1,128]{3,2,1,0:T(1,128)S(1)}, f32[3,16,1,128]{3,2,1,0:T(1,128)S(1)}, u32[]{:S(2)}, u32[]{:S(2)}) collective-permute-start(f32[3,16,1,128]{3,2,1,0:T(1,128)S(1)} %get-tuple-element.78), channel_id=1, source_target_pairs={{0,1},{1,2},{2,3},{3,4},{4,5},{5,6},{6,7},{7,0},{8,9},{9,10},{10,1... | collective-permute-start | bytes 73736 | tf_op jit(solution)/shard_map/ppermute | solution.py:39
  175.8 5.3 %collective-permute-start.7 = (f32[3,16,1,128]{3,2,1,0:T(1,128)}, f32[3,16,1,128]{3,2,1,0:T(1,128)}, u32[]{:S(2)}, u32[]{:S(2)}) collective-permute-start(f32[3,16,1,128]{3,2,1,0:T(1,128)} %get-tuple-element.77), channel_id=1, source_target_pairs={{1,0},{2,1},{3,2},{4,3},{5,4},{6,5},{7,6},{0,7},{9,8},{10,9},{11,1... | collective-permute-start | bytes 73736 | tf_op jit(solution)/shard_map/ppermute | solution.py:40
  (70 other events, 269.9 us)
